TPU v7x, 256 devices: a whole 4x4x8 slice. The times are simulated.
256 devices in a mesh: member: 32 (over x, y, core), grid: 8 (over z).
Axes of the slice: x: 4, y: 4, z: 8, core: 2. Of those that a mesh axis runs over, the one named last changes fastest.
Arguments:
- prior_ensemble: bfloat16 [512, 48, 32768], P('member', None, 'grid'), may hold values from -6 to 6
- measured_location: int32 [8, 32, 128], P('grid', 'member'), may hold values from 0 to 6143
- measured_tally: int32 [8, 32], P('grid', 'member'), may hold values from 32 to 128, as said below
- measured_reading: float32 [8, 32, 128], P('grid', 'member'), may hold values from -6 to 6
- measured_noise_sigma: float32 [8, 32, 128], P('grid', 'member'), may hold values from 0.5 to 20, as said below
Outputs:
- analysis: bfloat16 [512, 48, 32768], P('member', None, 'grid')
Inputs may be any that keep to these rules, and one draw needn't show every extreme that they name: `measured_location`: cell of the observation within its block of 48 rows and 128 columns. `measured_tally`: some block in every draw uses all 128 slots. `measured_noise_sigma`: positive error deviations.
All inputs are finite; a program needn't handle non-finite values.
Results may differ from a plain program's by a relative error of at most 0.0058.
Values may be sent and summed in bfloat16 or wider, within the bound.
A program may use at most 128 MiB of HBM per device.

v0:
```python
import jax
import jax.numpy as jnp
from jax import lax
from jax.sharding import PartitionSpec as P

HIGHEST_PRECISION = lax.Precision.HIGHEST


def whiten(hx_values, values, errors, obs_total):
    hx_float = hx_values.astype(jnp.float32)
    hx_mean = jnp.mean(hx_float, axis=0)
    usable = (jnp.arange(hx_values.shape[1], dtype=jnp.int32) < obs_total).astype(jnp.float32)
    scale_obs = usable / errors
    whitened = (hx_float - hx_mean) * scale_obs
    innovation = (values - hx_mean) * scale_obs
    return (whitened, innovation)


def transform_matrix(gram_total, drive_vector):
    members = gram_total.shape[0]
    identity = jnp.eye(members, dtype=jnp.float32)
    system = (members - 1.0) * identity + gram_total
    factor_low = jnp.linalg.cholesky(system)
    inverse = jax.scipy.linalg.solve_triangular(factor_low, identity, lower=True)
    inner = jnp.dot(inverse, drive_vector, precision=HIGHEST_PRECISION)
    mean_weight = jnp.dot(inverse.T, inner, precision=HIGHEST_PRECISION)
    spread = jnp.sqrt(members - 1.0) * inverse.T
    return (mean_weight[:, None] + spread).astype(jnp.bfloat16)


def local_sums(whitened, innovation):
    gram_local = lax.dot_general(
        whitened, whitened, (((1,), (1,)), ((), ())), precision=HIGHEST_PRECISION
    )
    drive_local = jnp.dot(whitened, innovation, precision=HIGHEST_PRECISION)
    return (gram_local, drive_local)


def reduce_gram(whitened, innovation):
    gram_local, drive_local = local_sums(whitened, innovation)
    gram_total, drive_vector = lax.psum((gram_local, drive_local), ("member", "grid"))
    return transform_matrix(gram_total, drive_vector)


def apply_block(state_block, transform):
    members, row_count, columns = state_block.shape
    flattened = state_block.reshape(members, row_count * columns)
    state_mean = jnp.mean(flattened.astype(jnp.float32), axis=0)
    anomalies = (flattened.astype(jnp.float32) - state_mean).astype(jnp.bfloat16)
    increment = lax.dot_general(
        transform, anomalies, (((0,), (0,)), ((), ())), preferred_element_type=jnp.float32
    )
    return (state_mean + increment).astype(jnp.bfloat16).reshape(members, row_count, columns)


def local(
    prior_ensemble, measured_location, measured_tally, measured_reading, measured_noise_sigma
):
    values = measured_reading[0, 0]
    errors = measured_noise_sigma[0, 0]
    obs_total = measured_tally[0, 0]
    shard_profiles = lax.all_to_all(
        prior_ensemble, "member", split_axis=2, concat_axis=0, tiled=True
    )
    members, row_count, columns = shard_profiles.shape
    hx_values = jnp.take(
        shard_profiles.reshape(members, row_count * columns), measured_location[0, 0], axis=1
    )
    whitened, innovation = whiten(hx_values, values, errors, obs_total)
    transform = reduce_gram(whitened, innovation)
    updated = apply_block(shard_profiles, transform)
    return lax.all_to_all(updated, "member", split_axis=0, concat_axis=2, tiled=True)


def solution(mesh):
    in_specs = (
        P("member", None, "grid"),
        P("grid", "member", None),
        P("grid", "member"),
        P("grid", "member", None),
        P("grid", "member", None),
    )
    out_specs = P("member", None, "grid")
    return jax.shard_map(local, mesh=mesh, in_specs=in_specs, out_specs=out_specs, check_vma=False)
```

profile of v0, /device:TPU:1, one launch (start us, length us, event | category | flops | bytes accessed | tf_op | source)
XLA Modules:
  0.0 763.0 jit_solution(7519993507879228197)
XLA Ops:
  6.5 19.4 %copy.19 = bf16[16,48,4096]{1,0,2:T(8,128)(2,1)} copy(bf16[16,48,4096]{2,1,0:T(8,128)(2,1)} %param.5) | data formatting | bytes 12582912 | tf_op args[0]
  25.9 31.8 %reshape.139 = bf16[32,2,49152]{2,1,0:T(2,128)(2,1)} reshape(bf16[4096,16,48]{2,1,0:T(8,128)(2,1)} %bitcast.111) | data formatting | bytes 12582912
  57.7 8.8 %all-to-all-start = ((bf16[32,2,49152]{2,1,0:T(2,128)(2,1)}), bf16[32,2,49152]{2,1,0:T(2,128)(2,1)}, u32[]{:S(2)}, u32[]{:S(2)}) async-start(bf16[32,2,49152]{2,1,0:T(2,128)(2,1)} %reshape.139), calls=%async_computation | async-start | bytes 12582912 | tf_op jit(solution)/shard_map/all_to_all | solution.py:62
  67.8 1.1 fusion.12
  68.9 74.8 %all-to-all-done = bf16[32,2,49152]{2,1,0:T(2,128)(2,1)} async-done(((bf16[32,2,49152]{2,1,0:T(2,128)(2,1)}), bf16[32,2,49152]{2,1,0:T(2,128)(2,1)}, u32[]{:S(2)}, u32[]{:S(2)}) %all-to-all-start) | async-done | bytes 6291488 | tf_op jit(solution)/shard_map/all_to_all | solution.py:62
  143.7 27.6 %reshape.140 = bf16[4096,16,48]{2,1,0:T(8,128)(2,1)} reshape(bf16[32,2,49152]{2,1,0:T(2,128)(2,1)} %all-to-all-done) | data formatting | bytes 12582912
  171.3 18.8 %copy.20 = bf16[16,48,32,128]{3,1,0,2:T(8,128)(2,1)} copy(bf16[16,48,32,128]{1,0,3,2:T(8,128)(2,1)} %bitcast.110) | data formatting | bytes 12582912 | tf_op jit(solution)/shard_map/all_to_all | solution.py:62
  190.1 7.1 copy.44
  197.1 8.7 %copy.21 = bf16[512,6144]{0,1:T(8,128)(2,1)} copy(bf16[512,6144]{1,0:T(8,128)(2,1)} %bitcast.119) | data formatting | bytes 12582912 | tf_op jit(solution)/shard_map/reshape | solution.py:47
  205.8 4.5 gather_fusion
  210.5 2.2 fusion.20
  213.1 88.8 %psum.15 = f32[512]{0:T(512)S(1)} all-reduce(f32[512]{0:T(512)S(1)} %bitcast.121), channel_id=1, replica_groups=mesh['member'=32,'grid'=8] {'member','grid'}, use_global_device_ids=true, to_apply=%region_11.12 | all-reduce | flops 512 | bytes 4096 | tf_op jit(solution)/shard_map/psum | solution.py:41
  301.8 4.1 convert_reduce_fusion
  306.6 173.9 %all-reduce.3.cloned.1.call-done = f32[512,512]{0,1:T(8,128)} async-done(((f32[512,512]{0,1:T(8,128)}), f32[512,512]{0,1:T(8,128)}) %all-reduce.3.cloned.1.call-update) | async-done | bytes 1048592 | tf_op jit(solution)/shard_map/psum | solution.py:41
  480.5 1.3 select_add_fusion
  482.1 1.4 fusion.6
  483.6 11.7 %cholesky.107 = f32[128,128]{1,0:T(8,128)S(1)} custom-call(f32[128,128]{1,0:T(8,128)S(1)} %cholesky.269), custom_call_target="Cholesky" | custom-call | tf_op jit(solution)/shard_map/jit(cholesky)/cholesky | solution.py:23
  495.4 9.8 %custom-call.31 = f32[1,128,128]{1,2,0:T(8,128)S(1)} custom-call(f32[1,128,128]{2,1,0:T(8,128)S(1)} %get-tuple-element.36), custom_call_target="InvertDiagBlocksLowerTriangular" | custom-call | tf_op jit(solution)/shard_map/jit(cholesky)/cholesky | solution.py:23
  505.9 11.9 %cholesky.221 = f32[128,128]{1,0:T(8,128)S(1)} custom-call(f32[128,128]{1,0:T(8,128)S(1)} %cholesky.273), custom_call_target="Cholesky" | custom-call | tf_op jit(solution)/shard_map/jit(cholesky)/cholesky | solution.py:23
  518.1 9.8 %custom-call.32 = f32[1,128,128]{1,2,0:T(8,128)S(1)} custom-call(f32[1,128,128]{2,1,0:T(8,128)S(1)} %get-tuple-element.34), custom_call_target="InvertDiagBlocksLowerTriangular" | custom-call | tf_op jit(solution)/shard_map/jit(cholesky)/cholesky | solution.py:23
  528.5 1.6 convolution_subtract_fusion.4
  530.7 13.2 %cholesky.242 = f32[128,128]{1,0:T(8,128)} custom-call(f32[128,128]{1,0:T(8,128)} %cholesky.278), custom_call_target="Cholesky" | custom-call | tf_op jit(solution)/shard_map/jit(cholesky)/cholesky | solution.py:23
  543.9 1.5 select_reduce_fusion.1
  545.4 1.6 copy.28
  546.9 0.8 constant_dynamic-update-slice_fusion
  547.8 11.3 %custom-call.33 = f32[1,128,128]{1,2,0:T(8,128)} custom-call(f32[1,128,128]{2,1,0:T(8,128)} %get-tuple-element.32), custom_call_target="InvertDiagBlocksLowerTriangular" | custom-call | tf_op jit(solution)/shard_map/jit(cholesky)/cholesky | solution.py:23
  559.1 1.1 convolution_dynamic-update-slice_fusion.1
  560.2 1.3 convolution_subtract_fusion.5
  561.5 12.1 %cholesky.259 = f32[128,128]{1,0:T(8,128)S(1)} custom-call(f32[128,128]{1,0:T(8,128)S(1)} %convolution_subtract_fusion.5), custom_call_target="Cholesky" | custom-call | tf_op jit(solution)/shard_map/jit(cholesky)/cholesky | solution.py:23
  575.0 0.7 compare_reduce_fusion.3
  576.3 1.3 compare_reduce_fusion
  580.2 1.1 select_select_fusion
  581.3 0.7 triangular_solve.100
  582.0 14.5 %while.1 = (s32[]{:T(128)}, f32[512,512]{0,1:T(8,128)}, s32[4,2]{0,1:T(2,128)S(1)}, f32[4,128,128]{2,1,0:T(8,128)}, s32[]{:T(128)}) while((s32[]{:T(128)}, f32[512,512]{0,1:T(8,128)}, s32[4,2]{0,1:T(2,128)S(1)}, f32[4,128,128]{2,1,0:T(8,128)}, s32[]{:T(128)}) %tuple.25), condition=%wide.while_cond, body=%wide.while_body.sunk | while | flops 2 | bytes 393829 | solution.py:24
  582.7 2.2 dynamic-slice.7
  586.3 2.2 dynamic-slice.7
  590.0 2.2 dynamic-slice.7
  593.6 2.2 dynamic-slice.7
  596.5 40.1 %custom-call.34 = f32[4,128,128]{1,2,0:T(8,128)S(1)} custom-call(f32[4,128,128]{2,1,0:T(8,128)} %get-tuple-element.12), custom_call_target="InvertDiagBlocksLowerTriangular" | custom-call | tf_op jit(solution)/shard_map/jit(_solve_triangular)/triangular_solve | solution.py:24
  637.0 1.6 convolution_subtract_fusion.1
  639.0 2.2 convolution_subtract_fusion
  641.7 2.5 convolution_subtract_fusion.2
  644.6 1.0 convolution_bitcast_fusion
  646.3 6.7 fusion.1
  653.0 4.7 copy.38
  657.7 81.4 %all_to_all.33 = bf16[512,48,128]{2,1,0:T(8,128)(2,1)S(1)} all-to-all(bf16[512,48,128]{2,1,0:T(8,128)(2,1)S(1)} %bitcast.116), channel_id=1, replica_groups=mesh['member'=32,'grid'=8] {'member'}, dimensions={0} | all-to-all | bytes 12582912 | tf_op jit(solution)/shard_map/all_to_all | solution.py:72
  739.0 6.7 copy.45
  745.7 10.3 %all_to_all.30 = bf16[16,48,4096]{2,1,0:T(8,128)(2,1)} reshape(bf16[16,48,32,128]{3,2,1,0:T(8,128)(2,1)} %bitcast.118) | data formatting | bytes 12582912 | tf_op jit(solution)/shard_map/all_to_all | solution.py:72
  (68 shorter events, 14.1 us)
Async XLA Ops:
  57.6 10.1 %copy-start.3 = (s32[1,1,128]{2,1,0:T(1,128)S(1)}, s32[1,1,128]{2,1,0:T(1,128)}, u32[]{:S(2)}) copy-start(s32[1,1,128]{2,1,0:T(1,128)} %param.6) | copy-start | bytes 1540
  57.7 86.1 %all-to-all-start = ((bf16[32,2,49152]{2,1,0:T(2,128)(2,1)}), bf16[32,2,49152]{2,1,0:T(2,128)(2,1)}, u32[]{:S(2)}, u32[]{:S(2)}) async-start(bf16[32,2,49152]{2,1,0:T(2,128)(2,1)} %reshape.139), calls=%async_computation | async-start | bytes 12582912 | tf_op jit(solution)/shard_map/all_to_all | solution.py:62
  66.4 414.0 %all-reduce.3.cloned.1.call-start = ((), (), s32[]{:S(2)}) async-start(), calls=%async_computation.2 | async-start | bytes 2097152 | tf_op jit(solution)/shard_map/psum | solution.py:41
  197.1 13.3 %copy-start.2 = (f32[1,1,128]{2,1,0:T(1,128)S(1)}, f32[1,1,128]{2,1,0:T(1,128)}, u32[]{:S(2)}) copy-start(f32[1,1,128]{2,1,0:T(1,128)} %param.9) | copy-start | bytes 1540
  197.1 15.6 %copy-start.4 = (f32[1,1,128]{2,1,0:T(1,128)S(1)}, f32[1,1,128]{2,1,0:T(1,128)}, u32[]{:S(2)}) copy-start(f32[1,1,128]{2,1,0:T(1,128)} %param.8) | copy-start | bytes 1540
  483.6 44.5 %copy-start = (f32[512,512]{1,0:T(8,128)}, f32[512,512]{1,0:T(8,128)S(1)}, u32[]{:S(2)}) copy-start(f32[512,512]{1,0:T(8,128)S(1)} %fusion.6) | copy-start | bytes 3145732
  528.5 117.8 %slice-start = ((s8[6291456]{0:T(1024)(128)(4,1)}), s8[2097152]{0:T(1024)(128)(4,1)S(1)}, s32[]{:S(2)}) async-start(s8[6291456]{0:T(1024)(128)(4,1)} %bitcast.113), calls=%async_computation.3 | async-start | bytes 4194304
  580.2 66.1 %copy-start.1 = (f32[6144]{0:T(1024)S(1)}, f32[6144]{0:T(1024)}, u32[]{:S(2)}) copy-start(f32[6144]{0:T(1024)} %multiply_bitcast_fusion) | copy-start | bytes 73732
  638.6 7.7 %slice-start.1 = ((s8[6291456]{0:T(1024)(128)(4,1)}), s8[4194304]{0:T(1024)(128)(4,1)S(1)}, s32[]{:S(2)}) async-start(s8[6291456]{0:T(1024)(128)(4,1)} %bitcast.113), calls=%async_computation.4 | async-start | bytes 8388608
Sparse Core Ops, SparseCore 0:
  212.8 267.5 all-reduce.2
where the time goes:
time: 773 us; the launch traced here: 763 us
  waiting for transfers between devices  249 us (32%)
  blocking collectives  170 us (22%)
  local copies, waits for them, and re-layouts  158 us (20%)
  other arithmetic  136 us (18%)
  matrix products  23.9 us (3%)
  between operations  17.1 us (2%)
  starting transfers between devices  8.8 us (1%)
    psum x1, waiting for transfers between devices, reduce_gram(): lax.psum((gram_local, drive_local), ('member', 'grid'))  174 us
    unnamed x19, local copies, waits for them, and re-layouts  90.5 us
    psum x1, blocking collectives, reduce_gram(): lax.psum((gram_local, drive_local), ('member', 'grid'))  88.8 us
    another operation x15, other arithmetic, transform_matrix(): factor_low = jnp.linalg.cholesky(system)  85.3 us
    all_to_all x1, blocking collectives, local(): lax.all_to_all(updated, 'member', split_axis=0, concat_axis=2, tiled=True)  81.4 us
    all_to_all x1, waiting for transfers between devices, local(): lax.all_to_all(prior_ensemble, 'member', split_axis=2, concat_axis=0, til...  74.8 us
    another operation x3, other arithmetic, transform_matrix(): jax.scipy.linalg.solve_triangular(factor_low, identity, lower=True)  41.8 us
    all_to_all x1, local copies, waits for them, and re-layouts, local(): lax.all_to_all(prior_ensemble, 'member', split_axis=2, concat_axis=0, til...  18.8 us
  transfers between devices with their start and end apart: 2, of which 2 were waited for; matrix products, arithmetic and copies ran while one was open for 1% of the time, Pallas kernels for 0%

commit v1 on v0

--- a/solution.py
+++ b/solution.py
@@ -38,7 +38,7 @@
 
 def reduce_gram(whitened, innovation):
     gram_local, drive_local = local_sums(whitened, innovation)
-    gram_total, drive_vector = lax.psum((gram_local, drive_local), ("member", "grid"))
+    gram_total, drive_vector = lax.psum(lax.psum((gram_local, drive_local), "member"), "grid")
     return transform_matrix(gram_total, drive_vector)
 
 

time: 773 us -> 716 us (0.926)
  waiting for transfers between devices: 249 us -> 202 us
  blocking collectives: 170 us -> 160 us
    psum x1 -> x2, waiting for transfers between devices: 174 us -> 125 us  [the longest x1 125 us: reduce_gram(): lax.psum((gram_local, drive_local), 'member')]
    psum x1 -> x2, blocking collectives: 88.8 us -> 77 us  [the longest x1 62.7 us: reduce_gram(): lax.psum((gram_local, drive_local), 'member')]
  transfers between devices with their start and end apart: 2 -> 3, of which waited for: 2 -> 2; matrix products, arithmetic and copies ran while one was open for 1% -> 1% of each run, Pallas kernels for 0% -> 0%
where the time goes in v1:
time: 716 us; the launch traced here: 706 us
  waiting for transfers between devices  202 us (28%)
  blocking collectives  160 us (22%)
  local copies, waits for them, and re-layouts  158 us (22%)
  other arithmetic  136 us (19%)
  matrix products  23.9 us (3%)
  between operations  17.1 us (2%)
  starting transfers between devices  8.84 us (1%)
    psum x1, waiting for transfers between devices, reduce_gram(): lax.psum((gram_local, drive_local), 'member')  125 us
    unnamed x19, local copies, waits for them, and re-layouts  90.5 us
    another operation x15, other arithmetic, transform_matrix(): factor_low = jnp.linalg.cholesky(system)  85.2 us
    all_to_all x1, blocking collectives, local(): lax.all_to_all(updated, 'member', split_axis=0, concat_axis=2, tiled=True)  83.3 us
    all_to_all x1, waiting for transfers between devices, local(): lax.all_to_all(prior_ensemble, 'member', split_axis=2, concat_axis=0, til...  76.5 us
    psum x1, blocking collectives, reduce_gram(): lax.psum((gram_local, drive_local), 'member')  62.7 us
    another operation x3, other arithmetic, transform_matrix(): jax.scipy.linalg.solve_triangular(factor_low, identity, lower=True)  41.9 us
    all_to_all x1, local copies, waits for them, and re-layouts, local(): lax.all_to_all(prior_ensemble, 'member', split_axis=2, concat_axis=0, til...  18.8 us
  transfers between devices with their start and end apart: 3, of which 2 were waited for; matrix products, arithmetic and copies ran while one was open for 1% of the time, Pallas kernels for 0%

profile of v1, /device:TPU:1, one launch (start us, length us, event | category | flops | bytes accessed | tf_op | source)
XLA Modules:
  0.0 706.0 jit_solution(9476911310865595630)
XLA Ops:
  6.5 19.4 %copy.19 = bf16[16,48,4096]{1,0,2:T(8,128)(2,1)} copy(bf16[16,48,4096]{2,1,0:T(8,128)(2,1)} %param.5) | data formatting | bytes 12582912 | tf_op args[0]
  25.9 31.8 %reshape.139 = bf16[32,2,49152]{2,1,0:T(2,128)(2,1)} reshape(bf16[4096,16,48]{2,1,0:T(8,128)(2,1)} %bitcast.111) | data formatting | bytes 12582912
  57.7 8.8 %all-to-all-start = ((bf16[32,2,49152]{2,1,0:T(2,128)(2,1)}), bf16[32,2,49152]{2,1,0:T(2,128)(2,1)}, u32[]{:S(2)}, u32[]{:S(2)}) async-start(bf16[32,2,49152]{2,1,0:T(2,128)(2,1)} %reshape.139), calls=%async_computation | async-start | bytes 12582912 | tf_op jit(solution)/shard_map/all_to_all | solution.py:62
  67.2 76.5 %all-to-all-done = bf16[32,2,49152]{2,1,0:T(2,128)(2,1)} async-done(((bf16[32,2,49152]{2,1,0:T(2,128)(2,1)}), bf16[32,2,49152]{2,1,0:T(2,128)(2,1)}, u32[]{:S(2)}, u32[]{:S(2)}) %all-to-all-start) | async-done | bytes 6291488 | tf_op jit(solution)/shard_map/all_to_all | solution.py:62
  143.7 27.6 %reshape.140 = bf16[4096,16,48]{2,1,0:T(8,128)(2,1)} reshape(bf16[32,2,49152]{2,1,0:T(2,128)(2,1)} %all-to-all-done) | data formatting | bytes 12582912
  171.3 18.8 %copy.20 = bf16[16,48,32,128]{3,1,0,2:T(8,128)(2,1)} copy(bf16[16,48,32,128]{1,0,3,2:T(8,128)(2,1)} %bitcast.110) | data formatting | bytes 12582912 | tf_op jit(solution)/shard_map/all_to_all | solution.py:62
  190.1 7.1 %copy.44 = bf16[64,8,48,128]{3,1,2,0:T(8,128)(2,1)} copy(bf16[64,8,48,128]{3,2,1,0:T(8,128)(2,1)} %bitcast.112) | data formatting | bytes 12582912
  197.1 8.7 %copy.21 = bf16[512,6144]{0,1:T(8,128)(2,1)} copy(bf16[512,6144]{1,0:T(8,128)(2,1)} %bitcast.119) | data formatting | bytes 12582912 | tf_op jit(solution)/shard_map/reshape | solution.py:47
  205.8 4.5 gather_fusion
  210.5 2.2 fusion.20
  212.8 125.2 %all-reduce.4.cloned.1.call-done = f32[512,512]{0,1:T(8,128)} async-done(((f32[512,512]{0,1:T(8,128)}), f32[512,512]{0,1:T(8,128)}) %all-reduce.4.cloned.1.call-update) | async-done | bytes 1048592 | tf_op jit(solution)/shard_map/psum | solution.py:41
  338.6 1.1 fusion.12
  340.0 62.7 %psum.30 = f32[512]{0:T(512)S(1)} all-reduce(f32[512]{0:T(512)S(1)} %bitcast.121), channel_id=1, replica_groups=mesh['member'=32,'grid'=8] {'member'}, use_global_device_ids=true, to_apply=%region_12.13 | all-reduce | flops 512 | bytes 4096 | tf_op jit(solution)/shard_map/psum | solution.py:41
  402.8 14.3 %psum.31 = f32[512]{0:T(512)S(1)} all-reduce(f32[512]{0:T(512)S(1)} %psum.30), channel_id=1, replica_groups=mesh['member'=32,'grid'=8] {'grid'}, use_global_device_ids=true, to_apply=%region_13.14 | all-reduce | flops 512 | bytes 4096 | tf_op jit(solution)/shard_map/psum | solution.py:41
  417.1 4.1 convert_reduce_fusion
  421.8 1.3 select_add_fusion
  423.5 1.4 fusion.6
  424.9 11.7 %cholesky.107 = f32[128,128]{1,0:T(8,128)S(1)} custom-call(f32[128,128]{1,0:T(8,128)S(1)} %cholesky.269), custom_call_target="Cholesky" | custom-call | tf_op jit(solution)/shard_map/jit(cholesky)/cholesky | solution.py:23
  436.7 9.8 %custom-call.31 = f32[1,128,128]{1,2,0:T(8,128)S(1)} custom-call(f32[1,128,128]{2,1,0:T(8,128)S(1)} %get-tuple-element.36), custom_call_target="InvertDiagBlocksLowerTriangular" | custom-call | tf_op jit(solution)/shard_map/jit(cholesky)/cholesky | solution.py:23
  447.2 11.9 %cholesky.221 = f32[128,128]{1,0:T(8,128)S(1)} custom-call(f32[128,128]{1,0:T(8,128)S(1)} %cholesky.273), custom_call_target="Cholesky" | custom-call | tf_op jit(solution)/shard_map/jit(cholesky)/cholesky | solution.py:23
  459.5 9.8 %custom-call.32 = f32[1,128,128]{1,2,0:T(8,128)S(1)} custom-call(f32[1,128,128]{2,1,0:T(8,128)S(1)} %get-tuple-element.34), custom_call_target="InvertDiagBlocksLowerTriangular" | custom-call | tf_op jit(solution)/shard_map/jit(cholesky)/cholesky | solution.py:23
  469.8 1.6 convolution_subtract_fusion.4
  472.1 13.2 %cholesky.242 = f32[128,128]{1,0:T(8,128)} custom-call(f32[128,128]{1,0:T(8,128)} %cholesky.278), custom_call_target="Cholesky" | custom-call | tf_op jit(solution)/shard_map/jit(cholesky)/cholesky | solution.py:23
  485.2 1.5 select_reduce_fusion.1
  486.7 1.6 copy.28
  488.3 0.8 constant_dynamic-update-slice_fusion
  489.1 11.3 %custom-call.33 = f32[1,128,128]{1,2,0:T(8,128)} custom-call(f32[1,128,128]{2,1,0:T(8,128)} %get-tuple-element.32), custom_call_target="InvertDiagBlocksLowerTriangular" | custom-call | tf_op jit(solution)/shard_map/jit(cholesky)/cholesky | solution.py:23
  500.4 1.1 convolution_dynamic-update-slice_fusion.1
  501.5 1.3 convolution_subtract_fusion.5
  502.8 12.1 %cholesky.259 = f32[128,128]{1,0:T(8,128)S(1)} custom-call(f32[128,128]{1,0:T(8,128)S(1)} %convolution_subtract_fusion.5), custom_call_target="Cholesky" | custom-call | tf_op jit(solution)/shard_map/jit(cholesky)/cholesky | solution.py:23
  516.3 0.7 compare_reduce_fusion.3
  517.7 1.3 compare_reduce_fusion
  521.4 1.2 select_select_fusion
  523.3 14.2 %while.1 = (s32[]{:T(128)}, f32[512,512]{0,1:T(8,128)}, s32[4,2]{0,1:T(2,128)S(1)}, f32[4,128,128]{2,1,0:T(8,128)}, s32[]{:T(128)}) while((s32[]{:T(128)}, f32[512,512]{0,1:T(8,128)}, s32[4,2]{0,1:T(2,128)S(1)}, f32[4,128,128]{2,1,0:T(8,128)}, s32[]{:T(128)}) %tuple.25), condition=%wide.while_cond, body=%wide.while_body.sunk | while | flops 2 | bytes 393829 | solution.py:24
  523.9 2.2 dynamic-slice.7
  527.5 2.2 dynamic-slice.7
  531.0 2.2 dynamic-slice.7
  534.6 2.2 dynamic-slice.7
  537.5 40.1 %custom-call.34 = f32[4,128,128]{1,2,0:T(8,128)S(1)} custom-call(f32[4,128,128]{2,1,0:T(8,128)} %get-tuple-element.12), custom_call_target="InvertDiagBlocksLowerTriangular" | custom-call | tf_op jit(solution)/shard_map/jit(_solve_triangular)/triangular_solve | solution.py:24
  577.9 1.6 convolution_subtract_fusion.1
  580.0 2.3 convolution_subtract_fusion
  582.7 2.5 convolution_subtract_fusion.2
  585.6 1.0 convolution_bitcast_fusion
  587.3 6.7 fusion.1
  594.0 4.7 copy.38
  598.7 83.3 %all_to_all.33 = bf16[512,48,128]{2,1,0:T(8,128)(2,1)S(1)} all-to-all(bf16[512,48,128]{2,1,0:T(8,128)(2,1)S(1)} %bitcast.116), channel_id=1, replica_groups=mesh['member'=32,'grid'=8] {'member'}, dimensions={0} | all-to-all | bytes 12582912 | tf_op jit(solution)/shard_map/all_to_all | solution.py:72
  682.0 6.7 copy.45
  688.7 10.3 %all_to_all.30 = bf16[16,48,4096]{2,1,0:T(8,128)(2,1)} reshape(bf16[16,48,32,128]{3,2,1,0:T(8,128)(2,1)} %bitcast.118) | data formatting | bytes 12582912 | tf_op jit(solution)/shard_map/all_to_all | solution.py:72
  (72 shorter events, 14.7 us)
Async XLA Ops:
  57.6 9.5 %copy-start.3 = (s32[1,1,128]{2,1,0:T(1,128)S(1)}, s32[1,1,128]{2,1,0:T(1,128)}, u32[]{:S(2)}) copy-start(s32[1,1,128]{2,1,0:T(1,128)} %param.6) | copy-start | bytes 1540
  57.7 86.1 %all-to-all-start = ((bf16[32,2,49152]{2,1,0:T(2,128)(2,1)}), bf16[32,2,49152]{2,1,0:T(2,128)(2,1)}, u32[]{:S(2)}, u32[]{:S(2)}) async-start(bf16[32,2,49152]{2,1,0:T(2,128)(2,1)} %reshape.139), calls=%async_computation | async-start | bytes 12582912 | tf_op jit(solution)/shard_map/all_to_all | solution.py:62
  66.4 271.6 %all-reduce.4.cloned.1.call-start = ((), (), s32[]{:S(2)}) async-start(), calls=%async_computation.2 | async-start | bytes 2097152 | tf_op jit(solution)/shard_map/psum | solution.py:41
  197.1 13.3 %copy-start.2 = (f32[1,1,128]{2,1,0:T(1,128)S(1)}, f32[1,1,128]{2,1,0:T(1,128)}, u32[]{:S(2)}) copy-start(f32[1,1,128]{2,1,0:T(1,128)} %param.9) | copy-start | bytes 1540
  197.1 142.6 %copy-start.4 = (f32[1,1,128]{2,1,0:T(1,128)S(1)}, f32[1,1,128]{2,1,0:T(1,128)}, u32[]{:S(2)}) copy-start(f32[1,1,128]{2,1,0:T(1,128)} %param.8) | copy-start | bytes 1540
  212.7 209.1 %all-reduce.6.cloned.1.call-start = ((), (), s32[]{:S(2)}) async-start(), calls=%async_computation.3 | async-start | bytes 2097152 | tf_op jit(solution)/shard_map/psum | solution.py:41
  424.9 44.5 %copy-start = (f32[512,512]{1,0:T(8,128)}, f32[512,512]{1,0:T(8,128)S(1)}, u32[]{:S(2)}) copy-start(f32[512,512]{1,0:T(8,128)S(1)} %fusion.6) | copy-start | bytes 3145732
  469.8 117.5 %slice-start = ((s8[6291456]{0:T(1024)(128)(4,1)}), s8[2097152]{0:T(1024)(128)(4,1)S(1)}, s32[]{:S(2)}) async-start(s8[6291456]{0:T(1024)(128)(4,1)} %bitcast.113), calls=%async_computation.4 | async-start | bytes 4194304
  521.4 65.9 %copy-start.1 = (f32[6144]{0:T(1024)S(1)}, f32[6144]{0:T(1024)}, u32[]{:S(2)}) copy-start(f32[6144]{0:T(1024)} %multiply_bitcast_fusion) | copy-start | bytes 73732
  579.5 7.8 %slice-start.1 = ((s8[6291456]{0:T(1024)(128)(4,1)}), s8[4194304]{0:T(1024)(128)(4,1)S(1)}, s32[]{:S(2)}) async-start(s8[6291456]{0:T(1024)(128)(4,1)} %bitcast.113), calls=%async_computation.5 | async-start | bytes 8388608
Sparse Core Ops, SparseCore 0:
  212.8 125.1 all-reduce.3
  340.3 71.4 all-reduce.5
